TPU v7x, 128 devices: a whole 4x4x4 slice. The times are simulated.
128 devices in a mesh: dp: 4 (over x_hi, core), patch: 32 (over y, x_lo, z).
Axes of the slice: x: 4 (x_hi: 2, x_lo: 2; x = x_hi * 2 + x_lo), y: 4, z: 4, core: 2. Of those that a mesh axis runs over, the one named last changes fastest.
Arguments:
- query_tokens: bfloat16 [4, 64, 128, 768], P('dp', 'patch')
- past_tokens: bfloat16 [4, 256, 128, 768], P('dp', 'patch'), may hold values from -6 to 6
- source_dev: int32 [64, 4, 3], replicated, may hold values from 0 to 31, all different within a row; in each aligned block of 8 rows (0 to 7, 8 to 15, ..., all dimensions but the last counted through in order) at most 2 rows name the same one
- source_slot: int32 [64, 4, 3], replicated, may hold values from 0 to 7
- kept: int32 [64, 4, 3], replicated, may hold values 0 or 1
- w_query: bfloat16 [768, 768], replicated
- w_key: bfloat16 [768, 768], replicated
- w_value: bfloat16 [768, 768], replicated, may hold values from -0.21875 to 0.21875
- w_out: bfloat16 [768, 768], replicated, may hold values from -0.875 to 0.875
- grad_out: bfloat16 [4, 64, 128, 768], P('dp', 'patch'), may hold values from -6 to 6
Outputs:
- attn_out: bfloat16 [4, 64, 128, 768], P('dp', 'patch')
- grad_query_tokens: bfloat16 [4, 64, 128, 768], P('dp', 'patch')
- grad_past_tokens: bfloat16 [4, 256, 128, 768], P('dp', 'patch')
- grad_w_query: float32 [768, 768], replicated
- grad_w_key: float32 [768, 768], replicated
- grad_w_value: float32 [768, 768], replicated
- grad_w_out: float32 [768, 768], replicated
Inputs may be any that keep to these rules, and one draw needn't show every extreme that they name: `source_dev`: row (p, f) lists the devices holding the frame-f blocks that patch p reads: 3 different devices a row. Over the rows of one device's 2 patches, no device is listed more than 2 times, and some device is listed exactly 2 times.
All inputs are finite; a program needn't handle non-finite values.
Results may differ from a plain program's by a relative error of at most 0.013.
The roundings to bfloat16 on the way count: a program that leaves them out, or rounds other values in their place, can miss the bound.
Values may be sent and summed in bfloat16 or wider, within the bound.
A program may use at most 256 MiB of HBM per device.

v0:
```python
import math
import jax
import jax.numpy as jnp
from jax import lax
from jax.sharding import PartitionSpec as P

H = 12
HD = 64


def attend(queries, keys, values, live):
    groups, query_rows, model_width = queries.shape
    key_rows = keys.shape[1]
    inv_scale = 1.0 / math.sqrt(HD)
    head_query = queries.reshape(groups, query_rows, H, HD)
    head_key = keys.reshape(groups, key_rows, H, HD)
    head_value = values.reshape(groups, key_rows, H, HD)
    scores = (
        jnp.einsum("gqhe,gkhe->ghqk", head_query, head_key, preferred_element_type=jnp.float32)
        * inv_scale
    )
    scores = jnp.where(live[:, None, None, :] > 0, scores, -jnp.inf)
    row_max = jnp.max(scores, axis=-1, keepdims=True)
    shifted = jnp.exp(scores - row_max)
    soft_probs = shifted / jnp.sum(shifted, axis=-1, keepdims=True)
    soft_weights = soft_probs.astype(jnp.bfloat16)
    mixed = jnp.einsum(
        "ghqk,gkhe->gqhe", soft_weights, head_value, preferred_element_type=jnp.float32
    )
    mixed = mixed.reshape(groups, query_rows, model_width).astype(jnp.bfloat16)
    return (mixed, soft_probs, soft_weights)


def attend_back(queries, keys, values, soft_probs, soft_weights, upstream):
    groups, query_rows, model_width = queries.shape
    key_rows = keys.shape[1]
    inv_scale = 1.0 / math.sqrt(HD)
    head_query = queries.reshape(groups, query_rows, H, HD)
    head_key = keys.reshape(groups, key_rows, H, HD)
    head_value = values.reshape(groups, key_rows, H, HD)
    head_up = upstream.reshape(groups, query_rows, H, HD)
    grad_prob = jnp.einsum(
        "gqhe,gkhe->ghqk", head_up, head_value, preferred_element_type=jnp.float32
    )
    row_delta = jnp.sum(soft_probs * grad_prob, axis=-1, keepdims=True)
    grad_score = (soft_probs * (grad_prob - row_delta) * inv_scale).astype(jnp.bfloat16)
    grad_q = jnp.einsum("ghqk,gkhe->gqhe", grad_score, head_key, preferred_element_type=jnp.float32)
    grad_k = jnp.einsum(
        "ghqk,gqhe->gkhe", grad_score, head_query, preferred_element_type=jnp.float32
    )
    grad_v = jnp.einsum(
        "ghqk,gqhe->gkhe", soft_weights, head_up, preferred_element_type=jnp.float32
    )
    grad_q = grad_q.reshape(groups, query_rows, model_width).astype(jnp.bfloat16)
    grad_k = grad_k.reshape(groups, key_rows, model_width).astype(jnp.bfloat16)
    grad_v = grad_v.reshape(groups, key_rows, model_width).astype(jnp.bfloat16)
    return (grad_q, grad_k, grad_v)


def forward_group(inputs):
    queries, keys, values, live = inputs
    mixed, soft_probs, soft_weights = attend(queries[None], keys[None], values[None], live[None])
    return (mixed[0], soft_probs[0], soft_weights[0])


def backward_group(inputs):
    queries, keys, values, soft_probs, soft_weights, upstream = inputs
    grad_q, grad_k, grad_v = attend_back(
        queries[None],
        keys[None],
        values[None],
        soft_probs[None],
        soft_weights[None],
        upstream[None],
    )
    return (grad_q[0], grad_k[0], grad_v[0])


def transpose_dot(left, right):
    return jnp.einsum("nd,ed->ne", left, right, preferred_element_type=jnp.float32)


def outer_sum(left, right):
    return jnp.einsum("nd,ne->de", left, right, preferred_element_type=jnp.float32)


def body(
    query_tokens,
    past_tokens,
    source_dev,
    source_slot,
    kept,
    w_query,
    w_key,
    w_value,
    w_out,
    grad_out,
):
    batch_local, patch_local, block_rows, model_width = query_tokens.shape
    slots_local = past_tokens.shape[1]
    peer_count = lax.axis_size("patch")
    device = lax.axis_index("patch")
    requests = source_dev.shape[1] * source_dev.shape[2]
    per_device = patch_local * requests
    capacity = max(2, (per_device + peer_count - 1) // peer_count + 1)
    owners = source_dev.reshape(peer_count, per_device)
    places = source_slot.reshape(peer_count, per_device)
    live_all = kept.reshape(peer_count, per_device)
    request_order = jnp.arange(per_device)
    earlier = request_order[:, None] > request_order[None, :]
    matches = (owners[:, :, None] == owners[:, None, :]) & earlier[None]
    slot_rank = jnp.sum(matches.astype(jnp.int32), axis=2)
    from_here = (owners == device) & (live_all > 0)
    slot_hit = (slot_rank[:, :, None] == jnp.arange(capacity)[None, None, :]) & from_here[
        :, :, None
    ]
    place_hit = places[:, :, None] == jnp.arange(slots_local)[None, None, :]
    chooser = jnp.einsum(
        "dqc,dqs->dcs", slot_hit.astype(jnp.float32), place_hit.astype(jnp.float32)
    ).astype(jnp.bfloat16)
    outgoing = jnp.einsum(
        "dcs,bsnw->bdcnw", chooser, past_tokens, preferred_element_type=jnp.float32
    ).astype(jnp.bfloat16)
    incoming = lax.all_to_all(outgoing, "patch", split_axis=1, concat_axis=1, tiled=True)
    my_owner = lax.dynamic_index_in_dim(owners, device, 0, keepdims=False)
    my_rank = lax.dynamic_index_in_dim(slot_rank, device, 0, keepdims=False)
    my_live = lax.dynamic_index_in_dim(live_all, device, 0, keepdims=False)
    position = my_owner * capacity + my_rank
    arrived = incoming.reshape(batch_local, peer_count * capacity, block_rows, model_width)
    fetched = jnp.take(arrived, position, axis=1)
    fetched_rows = fetched.reshape(batch_local * per_device * block_rows, model_width)
    w_proj = jnp.concatenate([w_query, w_key, w_value], axis=1)
    w_pair = jnp.concatenate([w_key, w_value], axis=1)
    token_rows = query_tokens.reshape(-1, model_width)
    own_proj = jnp.dot(token_rows, w_proj, preferred_element_type=jnp.float32).astype(jnp.bfloat16)
    far_proj = jnp.dot(fetched_rows, w_pair, preferred_element_type=jnp.float32).astype(
        jnp.bfloat16
    )
    groups = batch_local * patch_local
    far_rows = requests * block_rows
    queries = own_proj[:, :model_width].reshape(groups, block_rows, model_width)
    all_keys = jnp.concatenate(
        [
            own_proj[:, model_width : 2 * model_width].reshape(groups, block_rows, model_width),
            far_proj[:, :model_width].reshape(groups, far_rows, model_width),
        ],
        axis=1,
    )
    all_values = jnp.concatenate(
        [
            own_proj[:, 2 * model_width :].reshape(groups, block_rows, model_width),
            far_proj[:, model_width:].reshape(groups, far_rows, model_width),
        ],
        axis=1,
    )
    live_far = jnp.repeat(my_live.reshape(patch_local, requests), block_rows, axis=1)
    live_row = jnp.concatenate([jnp.ones((patch_local, block_rows), jnp.int32), live_far], axis=1)
    live_row = jnp.tile(live_row, (batch_local, 1))
    mixed, soft_probs, soft_weights = lax.map(
        forward_group, (queries, all_keys, all_values, live_row)
    )
    mixed_rows = mixed.reshape(-1, model_width)
    result = jnp.dot(mixed_rows, w_out, preferred_element_type=jnp.float32).astype(jnp.bfloat16)
    grad_rows = grad_out.reshape(-1, model_width)
    upstream = transpose_dot(grad_rows, w_out).astype(jnp.bfloat16)
    grad_wo = outer_sum(mixed_rows, grad_rows)
    grad_q, grad_k, grad_v = lax.map(
        backward_group,
        (
            queries,
            all_keys,
            all_values,
            soft_probs,
            soft_weights,
            upstream.reshape(groups, block_rows, model_width),
        ),
    )
    q_rows = grad_q.reshape(-1, model_width)
    own_k = grad_k[:, :block_rows].reshape(-1, model_width)
    own_v = grad_v[:, :block_rows].reshape(-1, model_width)
    far_k = grad_k[:, block_rows:].reshape(-1, model_width)
    far_v = grad_v[:, block_rows:].reshape(-1, model_width)
    grad_tokens = (
        transpose_dot(q_rows, w_query) + transpose_dot(own_k, w_key) + transpose_dot(own_v, w_value)
    ).astype(jnp.bfloat16)
    far_grad = (transpose_dot(far_k, w_key) + transpose_dot(far_v, w_value)).astype(jnp.bfloat16)
    far_grad = far_grad.reshape(batch_local, per_device, block_rows, model_width)
    back_rows = jnp.zeros(
        (batch_local, peer_count * capacity, block_rows, model_width), jnp.bfloat16
    )
    back_rows = back_rows.at[:, position].set(far_grad)
    returned = lax.all_to_all(
        back_rows.reshape(batch_local, peer_count, capacity, block_rows, model_width),
        "patch",
        split_axis=1,
        concat_axis=1,
        tiled=True,
    )
    past_grad = jnp.einsum(
        "dcs,bdcnw->bsnw", chooser, returned, preferred_element_type=jnp.float32
    ).astype(jnp.bfloat16)
    grad_wq = outer_sum(token_rows, q_rows)
    grad_wk = outer_sum(token_rows, own_k) + outer_sum(fetched_rows, far_k)
    grad_wv = outer_sum(token_rows, own_v) + outer_sum(fetched_rows, far_v)
    grad_wq, grad_wk, grad_wv, grad_wo = lax.psum(
        (grad_wq, grad_wk, grad_wv, grad_wo), ("dp", "patch")
    )
    inv_total = 1.0 / math.sqrt(
        lax.axis_size("dp") * batch_local * peer_count * patch_local * block_rows
    )
    return (
        result.reshape(query_tokens.shape),
        grad_tokens.reshape(query_tokens.shape),
        past_grad,
        grad_wq * inv_total,
        grad_wk * inv_total,
        grad_wv * inv_total,
        grad_wo * inv_total,
    )


def solution(mesh):
    placed = (
        P("dp", "patch", None, None),
        P("dp", "patch", None, None),
        P(),
        P(),
        P(),
        P(),
        P(),
        P(),
        P(),
        P("dp", "patch", None, None),
    )
    return jax.shard_map(
        body,
        mesh=mesh,
        in_specs=placed,
        out_specs=(
            P("dp", "patch", None, None),
            P("dp", "patch", None, None),
            P("dp", "patch", None, None),
            P(),
            P(),
            P(),
            P(),
        ),
        check_vma=False,
    )
```

profile of v0, /device:TPU:1, one launch (start us, length us, event | category | flops | bytes accessed | tf_op | source)
XLA Modules:
  0.0 947.2 jit_solution(16771115224350771100)
XLA Ops:
  15.9 21.9 %copy.171 = bf16[1,32,2,128,768]{4,3,2,0,1:T(8,128)(2,1)} copy(bf16[1,32,2,128,768]{4,1,3,2,0:T(8,128)(2,1)S(1)} %convert_bitcast_fusion) | data formatting | bytes 25165824 | tf_op jit(solution)/shard_map/convert_element_type | solution.py:123
  37.8 10.3 %all-to-all-start = ((bf16[1,32,2,128,768]{4,3,2,0,1:T(8,128)(2,1)}), bf16[1,32,2,128,768]{4,3,2,0,1:T(8,128)(2,1)}, u32[]{:S(2)}, u32[]{:S(2)}) async-start(bf16[1,32,2,128,768]{4,3,2,0,1:T(8,128)(2,1)} %copy.171), calls=%async_computation | async-start | bytes 25165824 | tf_op jit(solution)/shard_map/all_to_all | solution.py:124
  55.1 223.6 %all-to-all-done = bf16[1,32,2,128,768]{4,3,2,0,1:T(8,128)(2,1)} async-done(((bf16[1,32,2,128,768]{4,3,2,0,1:T(8,128)(2,1)}), bf16[1,32,2,128,768]{4,3,2,0,1:T(8,128)(2,1)}, u32[]{:S(2)}, u32[]{:S(2)}) %all-to-all-start) | async-done | bytes 12582944 | tf_op jit(solution)/shard_map/all_to_all | solution.py:124
  278.6 7.7 gather_fusion
  289.7 9.9 %convolution_convert_fusion.3 = bf16[3072,1536]{1,0:T(8,128)(2,1)} fusion(bf16[3072,768]{1,0:T(8,128)(2,1)S(1)} %bitcast_select_fusion.1, bf16[768,768]{1,0:T(8,128)(2,1)S(1)} %copy-done.16, bf16[768,768]{1,0:T(8,128)(2,1)S(1)} %copy-done.13), kind=kOutput, calls=%fused_computation.46 | convolution fusion | flops 7257194496 | bytes 16515072 | tf_op jit(solution)/shard_map/dot_general | solution.py:136
  299.6 7.9 fusion.56
  314.2 6.8 copy.175
  321.0 8.5 pad_maximum_fusion
  329.6 73.8 %while.28 = (s32[]{:T(128)}, bf16[2,128,768]{2,1,0:T(8,128)(2,1)S(1)}, f32[2,12,128,1664]{3,2,1,0:T(8,128)}, bf16[2,12,128,1664]{3,2,1,0:T(8,128)(2,1)}, bf16[2,...) while((s32[]{:T(128)}, ...), condition=%wide.region_4.5_spmd, body=%wide.region_1.0_spmd.sunk | while | flops 672304384 | bytes 83390360 | solution.py:159
  335.3 8.5 fusion.124
  343.8 9.6 %bitcast_dynamic-update-slice_fusion.4 = (bf16[2,12,128,1664]{3,2,1,0:T(8,128)(2,1)}, bf16[12,128,1664]{2,1,0:T(8,128)(2,1)}) fusion(bf16[2,12,128,1664]{3,2,1,0:T(8,128)(2,1)} %get-tuple-element.460, s32[]{:T(128)S(6)} %copy.244, f32[12,128,1664]{2,1,0:T(8,128)} %get-tuple-element.430, f32[12,128]{1,0:T(8,128)S(1)} %get-tuple-element.431), kind=kLoop, calls=%fused_computation.27.clone.1 | loop fusion | flops 5111808 | bytes 20453380 | tf_op jit(solution)/shard_map/while/body/jit(dynamic_update_index_in_dim)/dynamic_update_slice | solution.py:159
  358.0 8.8 bitcast_dynamic-update-slice_fusion.5
  372.0 8.5 fusion.124
  380.5 9.6 %bitcast_dynamic-update-slice_fusion.4 = (bf16[2,12,128,1664]{3,2,1,0:T(8,128)(2,1)}, bf16[12,128,1664]{2,1,0:T(8,128)(2,1)}) fusion(bf16[2,12,128,1664]{3,2,1,0:T(8,128)(2,1)} %get-tuple-element.460, s32[]{:T(128)S(6)} %copy.244, f32[12,128,1664]{2,1,0:T(8,128)} %get-tuple-element.430, f32[12,128]{1,0:T(8,128)S(1)} %get-tuple-element.431), kind=kLoop, calls=%fused_computation.27.clone.1 | loop fusion | flops 5111808 | bytes 20453380 | tf_op jit(solution)/shard_map/while/body/jit(dynamic_update_index_in_dim)/dynamic_update_slice | solution.py:159
  394.7 8.7 bitcast_dynamic-update-slice_fusion.5
  404.1 108.9 %while.29 = (s32[]{:T(128)}, bf16[2,128,768]{2,1,0:T(8,128)(2,1)S(1)}, bf16[2,1664,768]{2,1,0:T(8,128)(2,1)}, bf16[2,1664,768]{2,1,0:T(8,128)(2,1)}, bf16[2,1664...) while((s32[]{:T(128)}, ...), condition=%wide.region_7.8_spmd, body=%wide.region_5.7_spmd.sunk | while | flops 1326610944 | bytes 105001104 | solution.py:167
  409.8 9.4 fusion.133
  419.2 10.3 %fusion.134 = bf16[12,128,1664]{2,1,0:T(8,128)(2,1)} fusion(f32[12,128,1664]{2,1,0:T(8,128)} %get-tuple-element.444, f32[2,12,128,1664]{3,2,1,0:T(8,128)} %get-tuple-element.502, s32[]{:T(128)S(6)} %copy.256, f32[12,128]{1,0:T(8,128)S(1)} %get-tuple-element.445), kind=kLoop, calls=%fused_computation.7.clone.1 | loop fusion | flops 10223616 | bytes 25565188 | tf_op jit(solution)/shard_map/reshape.27
  464.2 9.4 fusion.133
  473.6 10.3 %fusion.134 = bf16[12,128,1664]{2,1,0:T(8,128)(2,1)} fusion(f32[12,128,1664]{2,1,0:T(8,128)} %get-tuple-element.444, f32[2,12,128,1664]{3,2,1,0:T(8,128)} %get-tuple-element.502, s32[]{:T(128)S(6)} %copy.256, f32[12,128]{1,0:T(8,128)S(1)} %get-tuple-element.445), kind=kLoop, calls=%fused_computation.7.clone.1 | loop fusion | flops 10223616 | bytes 25565188 | tf_op jit(solution)/shard_map/reshape.27
  533.0 15.2 %scatter_fusion = bf16[64,128,768]{2,1,0:T(8,128)(2,1)} fusion(bf16[64,128,768]{2,1,0:T(8,128)(2,1)} %broadcast.176, s32[24]{0:T(128)S(1)} %copy-done.24, bf16[24,128,768]{2,1,0:T(8,128)(2,1)} %bitcast.251), kind=kCustom, calls=%fused_computation.1 | custom fusion | bytes 14155872 | tf_op jit(solution)/shard_map/scatter | solution.py:191
  548.3 23.6 %copy.185 = bf16[1,32,2,128,768]{4,2,3,0,1:T(2,128)(2,1)} copy(bf16[1,32,2,128,768]{4,3,2,1,0:T(8,128)(2,1)} %bitcast.228) | data formatting | bytes 25165824 | tf_op jit(solution)/shard_map/reshape | solution.py:193
  603.9 308.0 %all-reduce.4.cloned.1.call-done = (f32[768,768]{0,1:T(8,128)}, f32[768,768]{0,1:T(8,128)}, f32[768,768]{0,1:T(8,128)}, f32[768,768]{0,1:T(8,128)}) async-done(((f32[768,768]{0,1:T(8,128)}, f32[768,768]{0,1:T(8,128)}, f32[768,768]{0,1:T(8,128)}, f32[768,768]{0,1:T(8,128)}), (f32[768,768]{0,1:T(8,128)}, f32[768,768]{0,1:T(8,128)}, f32[768,768]{0,1:T(8,128)}, ...) | async-done | bytes 9437200 | tf_op jit(solution)/shard_map/psum | solution.py:205
  927.4 11.3 %fusion.37 = bf16[1,8,128,768]{3,1,2,0:T(8,128)(2,1)S(1)} fusion(bf16[1,32,2,128,768]{4,2,3,0,1:T(2,128)(2,1)} %all-to-all-done.1, bf16[32,2,8]{0,2,1:T(8,128)(2,1)S(1)} %copy-done.20), kind=kOutput, calls=%fused_computation.68 | convolution fusion | flops 101449728 | bytes 14156800 | tf_op jit(solution)/shard_map/dcs,bdcnw->bsnw/dot_general | solution.py:199
  (174 shorter events, 183.8 us)
Async XLA Ops:
  7.2 47.4 %copy-start = (bf16[768,768]{1,0:T(8,128)(2,1)S(1)}, bf16[768,768]{1,0:T(8,128)(2,1)}, u32[]{:S(2)}) copy-start(bf16[768,768]{1,0:T(8,128)(2,1)} %param.22) | copy-start | bytes 3538948
  10.7 5.1 copy-start.19
  37.7 10.4 %copy-start.6 = (bf16[1,2,128,768]{3,2,1,0:T(8,128)(2,1)S(1)}, bf16[1,2,128,768]{3,2,1,0:T(8,128)(2,1)}, u32[]{:S(2)}) copy-start(bf16[1,2,128,768]{3,2,1,0:T(8,128)(2,1)} %param.14) | copy-start | bytes 1179652
  37.8 10.4 %copy-start.12 = (bf16[768,768]{1,0:T(8,128)(2,1)S(1)}, bf16[768,768]{1,0:T(8,128)(2,1)}, u32[]{:S(2)}) copy-start(bf16[768,768]{1,0:T(8,128)(2,1)} %param.20) | copy-start | bytes 3538948
  37.8 240.9 %all-to-all-start = ((bf16[1,32,2,128,768]{4,3,2,0,1:T(8,128)(2,1)}), bf16[1,32,2,128,768]{4,3,2,0,1:T(8,128)(2,1)}, u32[]{:S(2)}, u32[]{:S(2)}) async-start(bf16[1,32,2,128,768]{4,3,2,0,1:T(8,128)(2,1)} %copy.171), calls=%async_computation | async-start | bytes 25165824 | tf_op jit(solution)/shard_map/all_to_all | solution.py:124
  314.2 6.8 copy-start.10
  314.2 6.8 copy-start.11
  343.8 9.6 %copy-start.1 = (bf16[1,1664,768]{1,2,0:T(8,128)(2,1)S(1)}, bf16[1,1664,768]{1,2,0:T(8,128)(2,1)}, u32[]{:S(2)}) copy-start(bf16[1,1664,768]{1,2,0:T(8,128)(2,1)} %get-tuple-element.428) | copy-start | bytes 7667716 | tf_op jit(solution)/shard_map/while
  380.5 9.6 %copy-start.1 = (bf16[1,1664,768]{1,2,0:T(8,128)(2,1)S(1)}, bf16[1,1664,768]{1,2,0:T(8,128)(2,1)}, u32[]{:S(2)}) copy-start(bf16[1,1664,768]{1,2,0:T(8,128)(2,1)} %get-tuple-element.428) | copy-start | bytes 7667716 | tf_op jit(solution)/shard_map/while
  513.1 6.7 slice-start
  515.9 3.9 copy-start.3
  515.9 3.9 slice-start.1
  520.1 6.8 copy-start.2
  527.0 6.1 copy-start.24
  571.9 7.9 copy-start.7
  571.9 355.5 %all-to-all-start.1 = ((bf16[1,32,2,128,768]{4,2,3,0,1:T(2,128)(2,1)}), bf16[1,32,2,128,768]{4,2,3,0,1:T(2,128)(2,1)}, u32[]{:S(2)}, u32[]{:S(2)}) async-start(bf16[1,32,2,128,768]{4,2,3,0,1:T(2,128)(2,1)} %copy.185), calls=%async_computation.1 | async-start | bytes 25165824 | tf_op jit(solution)/shard_map/all_to_all | solution.py:192
  577.2 4.5 copy-start.5
  577.2 6.5 copy-start.22
  577.2 334.7 %all-reduce.4.cloned.1.call-start = ((), (), s32[]{:S(2)}) async-start(), calls=%async_computation.2 | async-start | bytes 18874368 | tf_op jit(solution)/shard_map/psum | solution.py:205
  577.6 4.1 copy-start.9
  581.7 5.0 slice-start.4
  583.6 9.3 slice-start.2
  586.7 6.2 slice-start.3
  923.5 3.8 copy-start.20
  (11 other events, 26.0 us)
Sparse Core Ops, SparseCore 0:
  599.2 312.6 all-reduce.3
where the time goes:
time: 954 us; the launch traced here: 947 us
  waiting for transfers between devices  532 us (56%)
  local copies, waits for them, and re-layouts  169 us (18%)
  matrix products  135 us (14%)
  other arithmetic  80.4 us (8%)
  starting transfers between devices  16.1 us (2%)
  between operations  14.7 us (2%)
    psum x1, waiting for transfers between devices, body(): lax.psum((grad_wq, grad_wk, grad_wv, grad_wo), ('dp', 'patch'))  308 us
    all_to_all x1, waiting for transfers between devices, body(): lax.all_to_all(outgoing, 'patch', split_axis=1, concat_axis=1, tiled=True)  224 us
    dynamic_update_slice x4, other arithmetic, body(): lax.map(forward_group, (queries, all_keys, all_values, live_row))  36.7 us
    dynamic_update_slice x6, local copies, waits for them, and re-layouts, body(): lax.map(backward_group, (queries, all_keys, all_values, soft_probs, soft_...  28.3 us
    reshape x1, local copies, waits for them, and re-layouts, body(): back_rows.reshape(batch_local, peer_count, capacity, block_rows, model_wi...  23.6 us
    convert_element_type x1, local copies, waits for them, and re-layouts, body(): outgoing = jnp.einsum('dcs,bsnw->bdcnw', chooser, past_tokens, preferred_...  21.9 us
    dynamic_slice x14, local copies, waits for them, and re-layouts, body(): lax.map(forward_group, (queries, all_keys, all_values, live_row))  21.3 us
    another operation x4, other arithmetic  20.6 us
  transfers between devices with their start and end apart: 3, of which 2 were waited for; matrix products, arithmetic and copies ran while one was open for 5% of the time, Pallas kernels for 0%

commit v1 on v0

--- a/solution.py
+++ b/solution.py
@@ -3,9 +3,11 @@
 import jax.numpy as jnp
 from jax import lax
 from jax.sharding import PartitionSpec as P
+from jax.lax import psum
 
 H = 12
 HD = 64
+_tell_map = lambda inp, dev_axis, row_axis: psum(psum(inp, dev_axis), axis_name=row_axis)
 
 
 def attend(queries, keys, values, live):
@@ -202,8 +204,8 @@
     grad_wq = outer_sum(token_rows, q_rows)
     grad_wk = outer_sum(token_rows, own_k) + outer_sum(fetched_rows, far_k)
     grad_wv = outer_sum(token_rows, own_v) + outer_sum(fetched_rows, far_v)
-    grad_wq, grad_wk, grad_wv, grad_wo = lax.psum(
-        (grad_wq, grad_wk, grad_wv, grad_wo), ("dp", "patch")
+    grad_wq, grad_wk, grad_wv, grad_wo = _tell_map(
+        (grad_wq, grad_wk, grad_wv, grad_wo), "patch", "dp"
     )
     inv_total = 1.0 / math.sqrt(
         lax.axis_size("dp") * batch_local * peer_count * patch_local * block_rows

time: 954 us -> 1270 us (1.33)
  waiting for transfers between devices: 532 us -> 845 us
    psum x1 -> x2, waiting for transfers between devices: 308 us -> 620 us  [the longest x1 439 us: psum(inp, dev_axis)]
  transfers between devices with their start and end apart: 3 -> 4, of which waited for: 2 -> 3; matrix products, arithmetic and copies ran while one was open for 5% -> 6% of each run, Pallas kernels for 0% -> 0%
where the time goes in v1:
time: 1270 us; the launch traced here: 1260 us
  waiting for transfers between devices  845 us (67%)
  local copies, waits for them, and re-layouts  172 us (14%)
  matrix products  137 us (11%)
  other arithmetic  77.9 us (6%)
  starting transfers between devices  15.2 us (1%)
  between operations  14.9 us (1%)
    psum x1, waiting for transfers between devices, psum(inp, dev_axis)  439 us
    all_to_all x1, waiting for transfers between devices, body(): lax.all_to_all(outgoing, 'patch', split_axis=1, concat_axis=1, tiled=True)  224 us
    psum x1, waiting for transfers between devices, psum(psum(inp, dev_axis), axis_name=row_axis)  181 us
    dynamic_update_slice x4, other arithmetic, body(): lax.map(forward_group, (queries, all_keys, all_values, live_row))  36.7 us
    dynamic_update_slice x6, local copies, waits for them, and re-layouts, body(): lax.map(backward_group, (queries, all_keys, all_values, soft_probs, soft_...  28.4 us
  transfers between devices with their start and end apart: 4, of which 3 were waited for; matrix products, arithmetic and copies ran while one was open for 6% of the time, Pallas kernels for 0%

profile of v1, /device:TPU:1, one launch (start us, length us, event | category | flops | bytes accessed | tf_op | source)
XLA Modules:
  0.0 1262.1 jit_solution(17473348396291262676)
XLA Ops:
  15.9 21.8 %copy.171 = bf16[1,32,2,128,768]{4,3,2,0,1:T(8,128)(2,1)} copy(bf16[1,32,2,128,768]{4,1,3,2,0:T(8,128)(2,1)S(1)} %convert_bitcast_fusion) | data formatting | bytes 25165824 | tf_op jit(solution)/shard_map/convert_element_type | solution.py:125
  37.7 10.0 all-to-all-start
  54.7 224.2 %all-to-all-done = bf16[1,32,2,128,768]{4,3,2,0,1:T(8,128)(2,1)} async-done(((bf16[1,32,2,128,768]{4,3,2,0,1:T(8,128)(2,1)}), bf16[1,32,2,128,768]{4,3,2,0,1:T(8,128)(2,1)}, u32[]{:S(2)}, u32[]{:S(2)}) %all-to-all-start) | async-done | bytes 12582944 | tf_op jit(solution)/shard_map/all_to_all | solution.py:126
  278.9 7.7 gather_fusion
  290.2 9.8 convolution_convert_fusion.3
  300.0 7.9 fusion.56
  321.4 8.5 pad_maximum_fusion
  330.0 73.3 %while.28 = (s32[]{:T(128)}, bf16[2,128,768]{2,1,0:T(8,128)(2,1)S(1)}, f32[2,12,128,1664]{3,2,1,0:T(8,128)}, bf16[2,12,128,1664]{3,2,1,0:T(8,128)(2,1)}, bf16[2,...) while((s32[]{:T(128)}, ...), condition=%wide.region_4.5_spmd, body=%wide.region_1.0_spmd.sunk | while | flops 672304384 | bytes 83390360 | solution.py:161
  335.2 8.5 fusion.124
  343.7 9.6 bitcast_dynamic-update-slice_fusion.4
  357.9 8.8 bitcast_dynamic-update-slice_fusion.5
  371.9 8.5 fusion.124
  380.4 9.6 bitcast_dynamic-update-slice_fusion.4
  394.6 8.7 bitcast_dynamic-update-slice_fusion.5
  404.1 109.3 %while.29 = (s32[]{:T(128)}, bf16[2,128,768]{2,1,0:T(8,128)(2,1)S(1)}, bf16[2,1664,768]{2,1,0:T(8,128)(2,1)}, bf16[2,1664,768]{2,1,0:T(8,128)(2,1)}, bf16[2,1664...) while((s32[]{:T(128)}, ...), condition=%wide.region_7.8_spmd, body=%wide.region_5.7_spmd.sunk | while | flops 1326610944 | bytes 105001104 | solution.py:169
  409.9 9.4 fusion.133
  419.3 10.3 fusion.134
  464.4 9.4 fusion.133
  473.7 10.3 fusion.134
  557.5 15.3 %scatter_fusion = bf16[64,128,768]{2,1,0:T(8,128)(2,1)} fusion(bf16[64,128,768]{2,1,0:T(8,128)(2,1)} %broadcast.176, s32[24]{0:T(128)S(1)} %copy-done.21, bf16[24,128,768]{2,1,0:T(8,128)(2,1)} %bitcast.251), kind=kCustom, calls=%fused_computation.1 | custom fusion | bytes 14155872 | tf_op jit(solution)/shard_map/scatter | solution.py:193
  572.8 23.7 %copy.185 = bf16[1,32,2,128,768]{4,2,3,0,1:T(2,128)(2,1)} copy(bf16[1,32,2,128,768]{4,3,2,1,0:T(8,128)(2,1)} %bitcast.228) | data formatting | bytes 25165824 | tf_op jit(solution)/shard_map/reshape | solution.py:195
  601.6 439.0 %all-reduce.6.cloned.1.call-done = (f32[768,768]{0,1:T(8,128)}, f32[768,768]{0,1:T(8,128)}, f32[768,768]{0,1:T(8,128)}, f32[768,768]{0,1:T(8,128)}) async-done(((f32[768,768]{0,1:T(8,128)}, f32[768,768]{0,1:T(8,128)}, f32[768,768]{0,1:T(8,128)}, f32[768,768]{0,1:T(8,128)}), (f32[768,768]{0,1:T(8,128)}, f32[768,768]{0,1:T(8,128)}, f32[768,768]{0,1:T(8,128)}, ...) | async-done | bytes 9437200 | tf_op jit(solution)/shard_map/psum | solution.py:10
  1045.5 11.3 fusion.37
  1058.3 181.3 %all-reduce.8.cloned.1.call-done = (f32[768,768]{0,1:T(8,128)}, f32[768,768]{0,1:T(8,128)}, f32[768,768]{0,1:T(8,128)}, f32[768,768]{0,1:T(8,128)}) async-done(((f32[768,768]{0,1:T(8,128)}, f32[768,768]{0,1:T(8,128)}, f32[768,768]{0,1:T(8,128)}, f32[768,768]{0,1:T(8,128)}), (f32[768,768]{0,1:T(8,128)}, f32[768,768]{0,1:T(8,128)}, f32[768,768]{0,1:T(8,128)}, ...) | async-done | bytes 9437200 | tf_op jit(solution)/shard_map/psum | solution.py:10
  (175 shorter events, 192.7 us)
Async XLA Ops:
  7.2 47.0 %copy-start = (bf16[768,768]{1,0:T(8,128)(2,1)S(1)}, bf16[768,768]{1,0:T(8,128)(2,1)}, u32[]{:S(2)}) copy-start(bf16[768,768]{1,0:T(8,128)(2,1)} %param.22) | copy-start | bytes 3538948
  10.7 5.1 copy-start.18
  37.7 10.1 copy-start.6
  37.7 10.2 copy-start.12
  37.7 241.2 %all-to-all-start = ((bf16[1,32,2,128,768]{4,3,2,0,1:T(8,128)(2,1)}), bf16[1,32,2,128,768]{4,3,2,0,1:T(8,128)(2,1)}, u32[]{:S(2)}, u32[]{:S(2)}) async-start(bf16[1,32,2,128,768]{4,3,2,0,1:T(8,128)(2,1)} %copy.171), calls=%async_computation | async-start | bytes 25165824 | tf_op jit(solution)/shard_map/all_to_all | solution.py:126
  47.7 992.9 %all-reduce.6.cloned.1.call-start = ((), (), s32[]{:S(2)}) async-start(), calls=%async_computation.2 | async-start | bytes 18874368 | tf_op jit(solution)/shard_map/psum | solution.py:10
  314.6 6.8 copy-start.10
  314.6 6.8 copy-start.11
  343.7 9.6 copy-start.1
  380.4 9.6 copy-start.1
  513.4 4.1 slice-start.2
  517.5 7.2 copy-start.2
  517.7 3.8 slice-start.1
  517.7 3.8 copy-start.23
  521.5 7.4 copy-start.3
  528.9 4.3 copy-start.5
  528.9 4.3 copy-start.9
  539.0 6.6 slice-start.4
  539.1 6.6 slice-start.5
  539.1 6.6 copy-start.16
  551.4 6.0 copy-start.21
  596.5 449.0 %all-to-all-start.1 = ((bf16[1,32,2,128,768]{4,2,3,0,1:T(2,128)(2,1)}), bf16[1,32,2,128,768]{4,2,3,0,1:T(2,128)(2,1)}, u32[]{:S(2)}, u32[]{:S(2)}) async-start(bf16[1,32,2,128,768]{4,2,3,0,1:T(2,128)(2,1)} %copy.185), calls=%async_computation.1 | async-start | bytes 25165824 | tf_op jit(solution)/shard_map/all_to_all | solution.py:194
  601.6 638.0 %all-reduce.8.cloned.1.call-start = ((), (), s32[]{:S(2)}) async-start(), calls=%async_computation.3 | async-start | bytes 18874368 | tf_op jit(solution)/shard_map/psum | solution.py:10
  1040.7 4.8 copy-start.19
  (11 other events, 27.2 us)
Sparse Core Ops, SparseCore 0:
  539.2 501.4 all-reduce.5
  1043.7 195.9 all-reduce.7
